TPU v7x, 256 devices: a whole 4x4x8 slice. The times are simulated.
256 devices in a mesh: gx: 16 (over z, core), gy: 16 (over y, x).
Axes of the slice: x: 4, y: 4, z: 8, core: 2. Of those that a mesh axis runs over, the one named last changes fastest.
Arguments:
- demand: float32 [16, 1024, 16384], P(None, 'gx', 'gy'), may hold values from -200 to 200, as said below
- initial: float32 [1024, 256], replicated, may hold values from -6 to 6
Outputs:
- factor: float32 [1024, 256], replicated
- core: float32 [256, 16, 16384], P('gx', None, 'gy')
Inputs may be any that keep to these rules, and one draw needn't show every extreme that they name: `demand`: Real-valued fluctuations of order one to a few, not all of one scale along x.
All inputs are finite; a program needn't handle non-finite values.
Results may differ from a plain program's by a relative error of at most 0.0003.
Values sent between devices are 32-bit elements; how exact they have to be, the bound alone decides.
No kernel may reach another device: no remote copies, remote signals or barrier semaphores. Data moves between devices by JAX's collectives and lax.ppermute only.
A program may use at most 128 MiB of HBM per device.

v0:
```python
import jax
import jax.numpy as jnp
from jax import lax
from jax.sharding import PartitionSpec as P

NY = 1024
L = 16
S = 16
ITERS = 3


def orthonormal(block):
    weights = jnp.dot(
        block.T, block, precision=lax.Precision.HIGHEST, preferred_element_type=jnp.float32
    )
    lower_factor = jnp.linalg.cholesky(weights)
    return lax.linalg.triangular_solve(
        lower_factor, block, left_side=False, lower=True, transpose_a=True
    )


def on_device(demand, initial):
    regrouped = lax.all_to_all(demand, "gx", split_axis=0, concat_axis=1, tiled=True)
    local_gram = jnp.einsum(
        "lxc,lzc->xz",
        regrouped,
        regrouped,
        precision=lax.Precision.HIGHEST,
        preferred_element_type=jnp.float32,
    )
    local_gram = local_gram * (1.0 / (L * S * NY))
    basis = initial
    gram = lax.psum(local_gram, ("gx", "gy"))
    for iteration in range(ITERS):
        basis = orthonormal(
            jnp.dot(
                gram, basis, precision=lax.Precision.HIGHEST, preferred_element_type=jnp.float32
            )
        )
    core_part = jnp.einsum(
        "xr,lxc->rlc",
        basis,
        regrouped,
        precision=lax.Precision.HIGHEST,
        preferred_element_type=jnp.float32,
    )
    core = lax.all_to_all(core_part, "gx", split_axis=0, concat_axis=1, tiled=True)
    return (basis, core)


def solution(mesh):
    in_specs = (P(None, "gx", "gy"), P())
    out_specs = (P(), P("gx", None, "gy"))
    return jax.shard_map(
        on_device, mesh=mesh, in_specs=in_specs, out_specs=out_specs, check_vma=False
    )
```

profile of v0, /device:TPU:1, one launch (start us, length us, event | category | flops | bytes accessed | tf_op | source)
XLA Modules:
  0.0 658.2 jit_solution(15279910534653061629)
XLA Ops:
  7.2 106.0 %all_to_all.27 = f32[16,64,1024]{2,1,0:T(8,128)S(1)} all-to-all(f32[16,64,1024]{2,1,0:T(8,128)} %param.5), channel_id=1, replica_groups=mesh['gx'=16,'gy'=16] {'gx'}, dimensions={0} | all-to-all | bytes 8388608 | tf_op jit(solution)/shard_map/all_to_all | solution.py:23
  113.2 1.9 copy-done.1
  115.1 14.7 %convolution_multiply_fusion = f32[1024,1024]{1,0:T(8,128)} fusion(f32[1024,1024]{1,0:T(8,128)S(1)} %bitcast.118), kind=kOutput, calls=%fused_computation.6 | convolution fusion | flops 12885950464 | bytes 8388608 | tf_op jit(solution)/shard_map/lxc,lzc->xz/dot_general | solution.py:24
  129.9 265.4 %all-reduce.3.cloned.1.call-done = f32[1024,1024]{1,0:T(8,128)} async-done(((f32[1024,1024]{1,0:T(8,128)}), f32[1024,1024]{1,0:T(8,128)}) %all-reduce.3.cloned.1.call-update) | async-done | bytes 4194320 | tf_op jit(solution)/shard_map/psum | solution.py:33
  395.3 5.4 fusion.45
  400.7 1.8 fusion.46
  402.8 11.7 %cholesky.172 = f32[128,128]{1,0:T(8,128)S(1)} custom-call(f32[128,128]{1,0:T(8,128)S(1)} %cholesky.270), custom_call_target="Cholesky" | custom-call | tf_op jit(solution)/shard_map/jit(cholesky)/cholesky | solution.py:16
  414.5 9.8 %custom-call.15 = f32[1,128,128]{1,2,0:T(8,128)S(1)} custom-call(f32[1,128,128]{2,1,0:T(8,128)S(1)} %get-tuple-element.72), custom_call_target="InvertDiagBlocksLowerTriangular" | custom-call | tf_op jit(solution)/shard_map/jit(cholesky)/cholesky | solution.py:16
  424.4 0.2 constant_dynamic-update-slice_fusion.5
  424.6 0.3 convolution_subtract_fusion.5
  424.8 11.7 %cholesky.189 = f32[128,128]{1,0:T(8,128)S(1)} custom-call(f32[128,128]{1,0:T(8,128)S(1)} %convolution_subtract_fusion.5), custom_call_target="Cholesky" | custom-call | tf_op jit(solution)/shard_map/jit(cholesky)/cholesky | solution.py:16
  436.6 0.7 compare_reduce_fusion.4
  439.0 3.7 while.6
  439.0 0.6 fusion.77
  439.6 1.3 bitcast_dynamic-update-slice_fusion.6
  440.9 0.6 fusion.77
  441.4 1.3 bitcast_dynamic-update-slice_fusion.6
  442.7 19.7 %custom-call.16 = f32[2,128,128]{1,2,0:T(8,128)S(1)} custom-call(f32[2,128,128]{2,1,0:T(8,128)S(1)} %get-tuple-element.24), custom_call_target="InvertDiagBlocksLowerTriangular" | custom-call | tf_op jit(solution)/shard_map/triangular_solve/custom-call.0 | solution.py:17
  462.4 0.6 fusion.12
  463.1 1.0 convolution_subtract_fusion.2
  464.1 0.6 fusion.25
  464.7 5.3 fusion
  470.0 1.8 fusion.47
  472.1 11.7 %cholesky.206 = f32[128,128]{1,0:T(8,128)S(1)} custom-call(f32[128,128]{1,0:T(8,128)S(1)} %cholesky.273), custom_call_target="Cholesky" | custom-call | tf_op jit(solution)/shard_map/jit(cholesky)/cholesky | solution.py:16
  483.8 9.8 %custom-call.17 = f32[1,128,128]{1,2,0:T(8,128)S(1)} custom-call(f32[1,128,128]{2,1,0:T(8,128)S(1)} %get-tuple-element.68), custom_call_target="InvertDiagBlocksLowerTriangular" | custom-call | tf_op jit(solution)/shard_map/jit(cholesky)/cholesky | solution.py:16
  493.9 0.3 convolution_subtract_fusion.4
  494.1 11.7 %cholesky.223 = f32[128,128]{1,0:T(8,128)S(1)} custom-call(f32[128,128]{1,0:T(8,128)S(1)} %convolution_subtract_fusion.4), custom_call_target="Cholesky" | custom-call | tf_op jit(solution)/shard_map/jit(cholesky)/cholesky | solution.py:16
  505.9 0.6 compare_reduce_fusion.2
  506.5 0.6 compare_reduce_fusion.3
  508.6 3.8 while.7
  508.6 0.6 fusion.78
  509.2 1.3 bitcast_dynamic-update-slice_fusion.7
  510.5 0.6 fusion.78
  511.1 1.3 bitcast_dynamic-update-slice_fusion.7
  512.4 19.7 %custom-call.18 = f32[2,128,128]{1,2,0:T(8,128)S(1)} custom-call(f32[2,128,128]{2,1,0:T(8,128)S(1)} %get-tuple-element.25), custom_call_target="InvertDiagBlocksLowerTriangular" | custom-call | tf_op jit(solution)/shard_map/triangular_solve/custom-call.0 | solution.py:17
  532.1 0.6 fusion.10
  532.8 1.0 convolution_subtract_fusion.1
  533.8 0.6 fusion.21
  534.4 5.5 fusion.4
  540.0 1.8 fusion.48
  542.0 11.7 %cholesky.240 = f32[128,128]{1,0:T(8,128)S(1)} custom-call(f32[128,128]{1,0:T(8,128)S(1)} %cholesky.276), custom_call_target="Cholesky" | custom-call | tf_op jit(solution)/shard_map/jit(cholesky)/cholesky | solution.py:16
  553.8 9.8 %custom-call.19 = f32[1,128,128]{1,2,0:T(8,128)S(1)} custom-call(f32[1,128,128]{2,1,0:T(8,128)S(1)} %get-tuple-element.64), custom_call_target="InvertDiagBlocksLowerTriangular" | custom-call | tf_op jit(solution)/shard_map/jit(cholesky)/cholesky | solution.py:16
  563.6 0.2 constant_dynamic-update-slice_fusion
  563.8 0.3 convolution_subtract_fusion.3
  564.1 11.7 %cholesky.257 = f32[128,128]{1,0:T(8,128)S(1)} custom-call(f32[128,128]{1,0:T(8,128)S(1)} %convolution_subtract_fusion.3), custom_call_target="Cholesky" | custom-call | tf_op jit(solution)/shard_map/jit(cholesky)/cholesky | solution.py:16
  575.8 0.6 compare_reduce_fusion
  576.5 0.6 compare_reduce_fusion.1
  578.4 0.3 select_select_fusion
  578.7 3.9 while.8
  578.7 0.6 fusion.79
  579.3 1.4 bitcast_dynamic-update-slice_fusion.8
  580.7 0.6 fusion.79
  581.3 1.4 bitcast_dynamic-update-slice_fusion.8
  582.6 19.7 %custom-call.20 = f32[2,128,128]{1,2,0:T(8,128)S(1)} custom-call(f32[2,128,128]{2,1,0:T(8,128)S(1)} %get-tuple-element.26), custom_call_target="InvertDiagBlocksLowerTriangular" | custom-call | tf_op jit(solution)/shard_map/triangular_solve/custom-call.0 | solution.py:17
  602.3 0.6 fusion.8
  603.0 1.0 convolution_subtract_fusion
  604.0 0.6 fusion.17
  604.6 5.7 convolution_bitcast_fusion
  610.3 2.1 copy.12
  612.4 7.6 %all-to-all-start.1 = ((f32[256,1,1024]{2,1,0:T(1,128)}), f32[256,1,1024]{2,1,0:T(1,128)}, u32[]{:S(2)}, u32[]{:S(2)}) async-start(f32[256,1,1024]{2,1,0:T(1,128)} %copy.12), calls=%async_computation.1 | async-start | bytes 2097152 | tf_op jit(solution)/shard_map/all_to_all | solution.py:47
  620.0 1.0 pad_maximum_fusion
  621.1 2.5 copy.14
  623.6 24.5 %all-to-all-done.1 = f32[256,1,1024]{2,1,0:T(1,128)} async-done(((f32[256,1,1024]{2,1,0:T(1,128)}), f32[256,1,1024]{2,1,0:T(1,128)}, u32[]{:S(2)}, u32[]{:S(2)}) %all-to-all-start.1) | async-done | bytes 1048608 | tf_op jit(solution)/shard_map/all_to_all | solution.py:47
  648.1 2.8 copy.16
  (37 shorter events, 1.4 us)
Async XLA Ops:
  7.2 388.1 %copy-start = (f32[1024,256]{1,0:T(8,128)S(1)}, f32[1024,256]{1,0:T(8,128)}, u32[]{:S(2)}) copy-start(f32[1024,256]{1,0:T(8,128)} %param.6) | copy-start | bytes 3145732
  7.2 388.1 %all-reduce.3.cloned.1.call-start = ((), (), s32[]{:S(2)}) async-start(), calls=%async_computation.2 | async-start | bytes 8388608 | tf_op jit(solution)/shard_map/psum | solution.py:33
  113.2 1.9 copy-start.1
  612.4 35.7 %all-to-all-start.1 = ((f32[256,1,1024]{2,1,0:T(1,128)}), f32[256,1,1024]{2,1,0:T(1,128)}, u32[]{:S(2)}, u32[]{:S(2)}) async-start(f32[256,1,1024]{2,1,0:T(1,128)} %copy.12), calls=%async_computation.1 | async-start | bytes 2097152 | tf_op jit(solution)/shard_map/all_to_all | solution.py:47
Sparse Core Ops, SparseCore 0:
  130.0 265.2 all-reduce.2
where the time goes:
time: 665 us; the launch traced here: 658 us
  waiting for transfers between devices  290 us (44%)
  other arithmetic  164 us (25%)
  blocking collectives  106 us (16%)
  matrix products  50.4 us (8%)
  local copies, waits for them, and re-layouts  21.3 us (3%)
  between operations  18.9 us (3%)
  starting transfers between devices  7.65 us (1%)
    psum x1, waiting for transfers between devices, on_device(): gram = lax.psum(local_gram, ('gx', 'gy'))  265 us
    all_to_all x1, blocking collectives, on_device(): lax.all_to_all(demand, 'gx', split_axis=0, concat_axis=1, tiled=True)  106 us
    another operation x20, other arithmetic, orthonormal(): lower_factor = jnp.linalg.cholesky(weights)  103 us
    another operation x8, other arithmetic, orthonormal(): lax.linalg.triangular_solve(lower_factor, block, left_side=False, lower=T...  60.6 us
    all_to_all x1, waiting for transfers between devices, on_device(): lax.all_to_all(core_part, 'gx', split_axis=0, concat_axis=1, tiled=True)  24.5 us
    dot_general x3, matrix products, on_device(): jnp.dot(gram, basis, precision=lax.Precision.HIGHEST, preferred_element_t...  16.3 us
    dot_general x1, matrix products, on_device(): jnp.einsum('lxc,lzc->xz', regrouped, regrouped, precision=lax.Precision.H...  14.7 us
  transfers between devices with their start and end apart: 2, of which 2 were waited for; matrix products, arithmetic and copies ran while one was open for 1% of the time, Pallas kernels for 0%

commit v1 on v0

--- a/solution.py
+++ b/solution.py
@@ -30,7 +30,7 @@
     )
     local_gram = local_gram * (1.0 / (L * S * NY))
     basis = initial
-    gram = lax.psum(local_gram, ("gx", "gy"))
+    gram = lax.psum(lax.psum(local_gram, "gx"), "gy")
     for iteration in range(ITERS):
         basis = orthonormal(
             jnp.dot(

time: 665 us -> 636 us (0.956)
  waiting for transfers between devices: 290 us -> 260 us
    psum x1 -> x2, waiting for transfers between devices: 265 us -> 235 us  [on_device(): gram = lax.psum(lax.psum(local_gram, 'gx'), 'gy')]
  transfers between devices with their start and end apart: 2 -> 3, of which waited for: 2 -> 3; matrix products, arithmetic and copies ran while one was open for 1% -> 1% of each run, Pallas kernels for 0% -> 0%
where the time goes in v1:
time: 636 us; the launch traced here: 628 us
  waiting for transfers between devices  260 us (41%)
  other arithmetic  164 us (26%)
  blocking collectives  106 us (17%)
  matrix products  50.4 us (8%)
  local copies, waits for them, and re-layouts  21.3 us (3%)
  between operations  19 us (3%)
  starting transfers between devices  8.12 us (1%)
    psum x2, waiting for transfers between devices, on_device(): gram = lax.psum(lax.psum(local_gram, 'gx'), 'gy')  235 us
    all_to_all x1, blocking collectives, on_device(): lax.all_to_all(demand, 'gx', split_axis=0, concat_axis=1, tiled=True)  106 us
    another operation x20, other arithmetic, orthonormal(): lower_factor = jnp.linalg.cholesky(weights)  103 us
    another operation x8, other arithmetic, orthonormal(): lax.linalg.triangular_solve(lower_factor, block, left_side=False, lower=T...  60.6 us
    all_to_all x1, waiting for transfers between devices, on_device(): lax.all_to_all(core_part, 'gx', split_axis=0, concat_axis=1, tiled=True)  24.5 us
    dot_general x3, matrix products, on_device(): jnp.dot(gram, basis, precision=lax.Precision.HIGHEST, preferred_element_t...  16.3 us
    dot_general x1, matrix products, on_device(): jnp.einsum('lxc,lzc->xz', regrouped, regrouped, precision=lax.Precision.H...  14.8 us
  transfers between devices with their start and end apart: 3, of which 3 were waited for; matrix products, arithmetic and copies ran while one was open for 1% of the time, Pallas kernels for 0%

profile of v1, /device:TPU:1, one launch (start us, length us, event | category | flops | bytes accessed | tf_op | source)
XLA Modules:
  0.0 628.5 jit_solution(16156951686608494834)
XLA Ops:
  7.2 106.0 %all_to_all.27 = f32[16,64,1024]{2,1,0:T(8,128)S(1)} all-to-all(f32[16,64,1024]{2,1,0:T(8,128)} %param.5), channel_id=1, replica_groups=mesh['gx'=16,'gy'=16] {'gx'}, dimensions={0} | all-to-all | bytes 8388608 | tf_op jit(solution)/shard_map/all_to_all | solution.py:23
  113.2 1.9 copy-done.1
  115.1 14.8 %convolution_multiply_fusion = f32[1024,1024]{1,0:T(8,128)} fusion(f32[1024,1024]{1,0:T(8,128)S(1)} %bitcast.118), kind=kOutput, calls=%fused_computation.6 | convolution fusion | flops 12885950464 | bytes 8388608 | tf_op jit(solution)/shard_map/lxc,lzc->xz/dot_general | solution.py:24
  130.0 117.9 %all-reduce.4.cloned.1.call-done = f32[1024,1024]{1,0:T(8,128)} async-done(((f32[1024,1024]{1,0:T(8,128)}), f32[1024,1024]{1,0:T(8,128)}) %all-reduce.4.cloned.1.call-update) | async-done | bytes 4194320 | tf_op jit(solution)/shard_map/psum | solution.py:33
  247.9 117.2 %all-reduce.6.cloned.1.call-done = f32[1024,1024]{1,0:T(8,128)} async-done(((f32[1024,1024]{1,0:T(8,128)}), f32[1024,1024]{1,0:T(8,128)}) %all-reduce.6.cloned.1.call-update) | async-done | bytes 4194320 | tf_op jit(solution)/shard_map/psum | solution.py:33
  365.2 5.4 fusion.45
  370.6 1.8 fusion.46
  372.6 11.7 %cholesky.172 = f32[128,128]{1,0:T(8,128)S(1)} custom-call(f32[128,128]{1,0:T(8,128)S(1)} %cholesky.270), custom_call_target="Cholesky" | custom-call | tf_op jit(solution)/shard_map/jit(cholesky)/cholesky | solution.py:16
  384.4 9.8 %custom-call.15 = f32[1,128,128]{1,2,0:T(8,128)S(1)} custom-call(f32[1,128,128]{2,1,0:T(8,128)S(1)} %get-tuple-element.72), custom_call_target="InvertDiagBlocksLowerTriangular" | custom-call | tf_op jit(solution)/shard_map/jit(cholesky)/cholesky | solution.py:16
  394.4 0.3 convolution_subtract_fusion.5
  394.7 11.7 %cholesky.189 = f32[128,128]{1,0:T(8,128)S(1)} custom-call(f32[128,128]{1,0:T(8,128)S(1)} %convolution_subtract_fusion.5), custom_call_target="Cholesky" | custom-call | tf_op jit(solution)/shard_map/jit(cholesky)/cholesky | solution.py:16
  406.4 0.7 compare_reduce_fusion.4
  408.8 3.7 while.6
  408.8 0.6 fusion.77
  409.4 1.3 bitcast_dynamic-update-slice_fusion.6
  410.7 0.6 fusion.77
  411.3 1.3 bitcast_dynamic-update-slice_fusion.6
  412.6 19.7 %custom-call.16 = f32[2,128,128]{1,2,0:T(8,128)S(1)} custom-call(f32[2,128,128]{2,1,0:T(8,128)S(1)} %get-tuple-element.24), custom_call_target="InvertDiagBlocksLowerTriangular" | custom-call | tf_op jit(solution)/shard_map/triangular_solve/custom-call.0 | solution.py:17
  432.3 0.6 fusion.12
  432.9 1.0 convolution_subtract_fusion.2
  433.9 0.6 fusion.25
  434.5 5.3 fusion
  439.9 1.8 fusion.47
  441.9 11.7 %cholesky.206 = f32[128,128]{1,0:T(8,128)S(1)} custom-call(f32[128,128]{1,0:T(8,128)S(1)} %cholesky.273), custom_call_target="Cholesky" | custom-call | tf_op jit(solution)/shard_map/jit(cholesky)/cholesky | solution.py:16
  453.7 9.8 %custom-call.17 = f32[1,128,128]{1,2,0:T(8,128)S(1)} custom-call(f32[1,128,128]{2,1,0:T(8,128)S(1)} %get-tuple-element.68), custom_call_target="InvertDiagBlocksLowerTriangular" | custom-call | tf_op jit(solution)/shard_map/jit(cholesky)/cholesky | solution.py:16
  463.5 0.2 constant_dynamic-update-slice_fusion.3
  463.7 0.3 convolution_subtract_fusion.4
  464.0 11.7 %cholesky.223 = f32[128,128]{1,0:T(8,128)S(1)} custom-call(f32[128,128]{1,0:T(8,128)S(1)} %convolution_subtract_fusion.4), custom_call_target="Cholesky" | custom-call | tf_op jit(solution)/shard_map/jit(cholesky)/cholesky | solution.py:16
  475.7 0.6 compare_reduce_fusion.2
  476.3 0.6 compare_reduce_fusion.3
  478.4 3.8 while.7
  478.4 0.6 fusion.78
  479.0 1.3 bitcast_dynamic-update-slice_fusion.7
  480.4 0.6 fusion.78
  481.0 1.3 bitcast_dynamic-update-slice_fusion.7
  482.3 19.7 %custom-call.18 = f32[2,128,128]{1,2,0:T(8,128)S(1)} custom-call(f32[2,128,128]{2,1,0:T(8,128)S(1)} %get-tuple-element.25), custom_call_target="InvertDiagBlocksLowerTriangular" | custom-call | tf_op jit(solution)/shard_map/triangular_solve/custom-call.0 | solution.py:17
  502.0 0.6 fusion.10
  502.6 1.0 convolution_subtract_fusion.1
  503.6 0.6 fusion.21
  504.2 5.5 fusion.4
  509.8 1.8 fusion.48
  511.8 11.7 %cholesky.240 = f32[128,128]{1,0:T(8,128)S(1)} custom-call(f32[128,128]{1,0:T(8,128)S(1)} %cholesky.276), custom_call_target="Cholesky" | custom-call | tf_op jit(solution)/shard_map/jit(cholesky)/cholesky | solution.py:16
  523.6 9.8 %custom-call.19 = f32[1,128,128]{1,2,0:T(8,128)S(1)} custom-call(f32[1,128,128]{2,1,0:T(8,128)S(1)} %get-tuple-element.64), custom_call_target="InvertDiagBlocksLowerTriangular" | custom-call | tf_op jit(solution)/shard_map/jit(cholesky)/cholesky | solution.py:16
  533.6 0.3 convolution_subtract_fusion.3
  533.9 11.7 %cholesky.257 = f32[128,128]{1,0:T(8,128)S(1)} custom-call(f32[128,128]{1,0:T(8,128)S(1)} %convolution_subtract_fusion.3), custom_call_target="Cholesky" | custom-call | tf_op jit(solution)/shard_map/jit(cholesky)/cholesky | solution.py:16
  545.6 0.6 compare_reduce_fusion
  546.3 0.6 compare_reduce_fusion.1
  548.2 0.3 select_select_fusion
  548.5 3.9 while.8
  548.5 0.6 fusion.79
  549.1 1.4 bitcast_dynamic-update-slice_fusion.8
  550.5 0.6 fusion.79
  551.1 1.4 bitcast_dynamic-update-slice_fusion.8
  552.5 19.7 %custom-call.20 = f32[2,128,128]{1,2,0:T(8,128)S(1)} custom-call(f32[2,128,128]{2,1,0:T(8,128)S(1)} %get-tuple-element.26), custom_call_target="InvertDiagBlocksLowerTriangular" | custom-call | tf_op jit(solution)/shard_map/triangular_solve/custom-call.0 | solution.py:17
  572.1 0.6 fusion.8
  572.8 1.0 convolution_subtract_fusion
  573.8 0.6 fusion.17
  574.4 5.7 convolution_bitcast_fusion
  580.1 2.1 copy.12
  582.2 8.0 %all-to-all-start.1 = ((f32[256,1,1024]{2,1,0:T(1,128)}), f32[256,1,1024]{2,1,0:T(1,128)}, u32[]{:S(2)}, u32[]{:S(2)}) async-start(f32[256,1,1024]{2,1,0:T(1,128)} %copy.12), calls=%async_computation.1 | async-start | bytes 2097152 | tf_op jit(solution)/shard_map/all_to_all | solution.py:47
  590.3 1.1 pad_maximum_fusion
  591.4 2.5 copy.14
  593.9 24.5 %all-to-all-done.1 = f32[256,1,1024]{2,1,0:T(1,128)} async-done(((f32[256,1,1024]{2,1,0:T(1,128)}), f32[256,1,1024]{2,1,0:T(1,128)}, u32[]{:S(2)}, u32[]{:S(2)}) %all-to-all-start.1) | async-done | bytes 1048608 | tf_op jit(solution)/shard_map/all_to_all | solution.py:47
  618.4 2.8 copy.16
  (40 shorter events, 1.7 us)
Async XLA Ops:
  7.2 358.0 %copy-start = (f32[1024,256]{1,0:T(8,128)S(1)}, f32[1024,256]{1,0:T(8,128)}, u32[]{:S(2)}) copy-start(f32[1024,256]{1,0:T(8,128)} %param.6) | copy-start | bytes 3145732
  7.2 240.7 %all-reduce.4.cloned.1.call-start = ((), (), s32[]{:S(2)}) async-start(), calls=%async_computation.2 | async-start | bytes 8388608 | tf_op jit(solution)/shard_map/psum | solution.py:33
  113.2 1.9 copy-start.1
  129.9 235.2 %all-reduce.6.cloned.1.call-start = ((), (), s32[]{:S(2)}) async-start(), calls=%async_computation.3 | async-start | bytes 8388608 | tf_op jit(solution)/shard_map/psum | solution.py:33
  582.2 36.1 %all-to-all-start.1 = ((f32[256,1,1024]{2,1,0:T(1,128)}), f32[256,1,1024]{2,1,0:T(1,128)}, u32[]{:S(2)}, u32[]{:S(2)}) async-start(f32[256,1,1024]{2,1,0:T(1,128)} %copy.12), calls=%async_computation.1 | async-start | bytes 2097152 | tf_op jit(solution)/shard_map/all_to_all | solution.py:47
Sparse Core Ops, SparseCore 0:
  130.0 117.7 all-reduce.3
  251.2 113.8 all-reduce.5
